TPU v7x, 256 devices: a whole 4x4x8 slice. The times are simulated.
256 devices in a mesh: tm: 64 (over z, x, core), col: 4 (over y).
Axes of the slice: x: 4, y: 4, z: 8, core: 2. Of those that a mesh axis runs over, the one named last changes fastest.
Arguments:
- couple: float32 [64, 1024, 1024], P('tm'), may hold values from -1 to 1
- free_term: float32 [64, 64, 1024], P('tm'), may hold values from -4 to 4
- slab_left: float32 [64, 4, 1024, 1024], P('tm', None, None, 'col'), may hold values from -0.125 to 0.125
- slab_right: float32 [64, 4, 1024, 1024], P('tm', None, None, 'col'), may hold values from -0.125 to 0.125
- arrow_rows: float32 [64, 64, 1024], P('tm', None, 'col'), may hold values from -0.0234375 to 0.0234375
- corner_base: float32 [64, 64], replicated, may hold values from -4 to 4
Outputs:
- boundary: float32 [64, 64, 1024], P('tm', None, 'col')
- slab_inverse: float32 [64, 4, 64, 1024], P('tm', None, None, 'col')
- corner: float32 [64, 64], replicated
All inputs are finite; a program needn't handle non-finite values.
Results may differ from a plain program's by a relative error of at most 0.00015.
Values sent between devices are 32-bit elements; how exact they have to be, the bound alone decides.
No kernel may reach another device: no remote copies, remote signals or barrier semaphores. Data moves between devices by JAX's collectives and lax.ppermute only.
A program may use at most 128 MiB of HBM per device.

v0:
```python
import jax
import jax.numpy as jnp
from jax import lax
from jax.sharding import PartitionSpec as P


def from_behind(array, axis, by):
    count = lax.axis_size(axis)
    pairs = [(i, i + by) for i in range(count) if 0 <= i + by < count]
    return lax.ppermute(array, axis, pairs)


def local(couple, free_term, slab_left, slab_right, arrow_rows, corner_base):
    highest = lax.Precision.HIGHEST
    transfer = couple[0]
    own_term = free_term[0]
    part_count = lax.axis_size("tm")
    col_count = lax.axis_size("col")
    col_index = lax.axis_index("col")
    col_width = transfer.shape[1] // col_count
    position = lax.axis_index("tm")

    def advance(counter, state):
        later_state = from_behind(state, "tm", -1)

        def update(incoming):
            return (
                jnp.dot(incoming, transfer, precision=highest, preferred_element_type=jnp.float32)
                + own_term
            )

        def keep_state(incoming):
            return state

        return lax.cond(part_count - 2 - position == counter, update, keep_state, later_state)

    boundary = lax.fori_loop(0, part_count - 1, advance, own_term)
    following = from_behind(boundary, "tm", -1)
    slab_blocks = jnp.einsum(
        "ab,kbc->kac", boundary, slab_left[0], precision=highest, preferred_element_type=jnp.float32
    )
    slab_blocks = slab_blocks + jnp.einsum(
        "ab,kbc->kac",
        following,
        slab_right[0],
        precision=highest,
        preferred_element_type=jnp.float32,
    )
    own_columns = lax.dynamic_slice_in_dim(boundary, col_index * col_width, col_width, 1)
    partial_value = jnp.dot(
        arrow_rows[0], own_columns.T, precision=highest, preferred_element_type=jnp.float32
    )
    corner = corner_base + lax.psum(partial_value, ("tm", "col"))
    return (own_columns[None], slab_blocks[None], corner)


def solution(mesh):
    placed = (
        P("tm", None, None),
        P("tm", None, None),
        P("tm", None, None, "col"),
        P("tm", None, None, "col"),
        P("tm", None, "col"),
        P(),
    )
    return jax.shard_map(
        local,
        mesh=mesh,
        in_specs=placed,
        out_specs=(P("tm", None, "col"), P("tm", None, None, "col"), P()),
        check_vma=False,
    )
```

profile of v0, /device:TPU:1, one launch (start us, length us, event | category | flops | bytes accessed | tf_op | source)
XLA Modules:
  0.0 790.8 jit_solution(10620637160481820337)
XLA Ops:
  1.6 669.1 %while.18 = (s32[]{:T(128)}, f32[64,1024]{1,0:T(8,128)S(1)}, s32[]{:T(128)}, f32[1024,1024]{1,0:T(8,128)}, f32[64,1024]{1,0:T(8,128)}, /*index=5*/s32[]{:T(128)}) while((s32[]{:T(128)}, f32[64,1024]{1,0:T(8,128)S(1)}, s32[]{:T(128)}, f32[1024,1024]{1,0:T(8,128)}, f32[64,1024]{1,0:T(8,128)}, /*index=5*/s32[]{:T(128)}) %tuple.60), condition=%wide.region_3.0_spmd, body=%wide.region_0.0_spmd.sunk | while | flops 805371904 | bytes 6029475 | solution.py:37
  114.0 7.9 collective-permute-done
  123.8 7.9 collective-permute-done
  133.5 7.9 collective-permute-done
  143.3 7.9 collective-permute-done
  153.1 7.9 collective-permute-done
  162.9 7.9 collective-permute-done
  172.7 7.9 collective-permute-done
  182.5 7.9 collective-permute-done
  192.3 7.9 collective-permute-done
  202.1 7.9 collective-permute-done
  211.9 7.9 collective-permute-done
  221.7 7.9 collective-permute-done
  231.4 7.9 collective-permute-done
  241.2 7.9 collective-permute-done
  251.0 7.9 collective-permute-done
  260.8 7.9 collective-permute-done
  270.6 7.9 collective-permute-done
  280.4 7.9 collective-permute-done
  290.2 7.9 collective-permute-done
  300.0 7.9 collective-permute-done
  309.8 7.9 collective-permute-done
  319.6 7.9 collective-permute-done
  329.3 7.9 collective-permute-done
  339.1 7.9 collective-permute-done
  348.9 7.9 collective-permute-done
  358.7 7.9 collective-permute-done
  368.5 7.9 collective-permute-done
  378.3 7.9 collective-permute-done
  388.1 7.9 collective-permute-done
  574.1 84.1 %collective-permute-done = f32[64,1024]{1,0:T(8,128)S(1)} collective-permute-done((f32[64,1024]{1,0:T(8,128)S(1)}, f32[64,1024]{1,0:T(8,128)S(1)}, u32[]{:S(2)}, u32[]{:S(2)}) %collective-permute-start) | collective-permute-done | bytes 262176 | tf_op jit(solution)/shard_map/while/body/eval_jaxpr/ppermute | solution.py:10
  674.2 107.5 %psum.7 = f32[64,64]{0,1:T(8,128)S(1)} all-reduce(f32[64,64]{0,1:T(8,128)S(1)} %convolution_bitcast_fusion), channel_id=1, replica_groups=mesh['tm'=64,'col'=4] {'tm','col'}, use_global_device_ids=true, to_apply=%region_4.0 | all-reduce | flops 4096 | bytes 32768 | tf_op jit(solution)/shard_map/psum | solution.py:53
  (176 shorter events, 374.3 us)
Async XLA Ops:
  112.0 9.8 %collective-permute-start = (f32[64,1024]{1,0:T(8,128)S(1)}, f32[64,1024]{1,0:T(8,128)S(1)}, u32[]{:S(2)}, u32[]{:S(2)}) collective-permute-start(f32[64,1024]{1,0:T(8,128)S(1)} %get-tuple-element.202), channel_id=1, source_target_pairs={{4,0},{8,4},{12,8},{16,12},{20,16},{24,20},{28,24},{32,28},{36,32}... | collective-permute-start | bytes 786440 | tf_op jit(solution)/shard_map/while/body/eval_jaxpr/ppermute | solution.py:10
  121.8 9.8 %collective-permute-start = (f32[64,1024]{1,0:T(8,128)S(1)}, f32[64,1024]{1,0:T(8,128)S(1)}, u32[]{:S(2)}, u32[]{:S(2)}) collective-permute-start(f32[64,1024]{1,0:T(8,128)S(1)} %get-tuple-element.202), channel_id=1, source_target_pairs={{4,0},{8,4},{12,8},{16,12},{20,16},{24,20},{28,24},{32,28},{36,32}... | collective-permute-start | bytes 786440 | tf_op jit(solution)/shard_map/while/body/eval_jaxpr/ppermute | solution.py:10
  131.6 9.8 %collective-permute-start = (f32[64,1024]{1,0:T(8,128)S(1)}, f32[64,1024]{1,0:T(8,128)S(1)}, u32[]{:S(2)}, u32[]{:S(2)}) collective-permute-start(f32[64,1024]{1,0:T(8,128)S(1)} %get-tuple-element.202), channel_id=1, source_target_pairs={{4,0},{8,4},{12,8},{16,12},{20,16},{24,20},{28,24},{32,28},{36,32}... | collective-permute-start | bytes 786440 | tf_op jit(solution)/shard_map/while/body/eval_jaxpr/ppermute | solution.py:10
  141.4 9.8 %collective-permute-start = (f32[64,1024]{1,0:T(8,128)S(1)}, f32[64,1024]{1,0:T(8,128)S(1)}, u32[]{:S(2)}, u32[]{:S(2)}) collective-permute-start(f32[64,1024]{1,0:T(8,128)S(1)} %get-tuple-element.202), channel_id=1, source_target_pairs={{4,0},{8,4},{12,8},{16,12},{20,16},{24,20},{28,24},{32,28},{36,32}... | collective-permute-start | bytes 786440 | tf_op jit(solution)/shard_map/while/body/eval_jaxpr/ppermute | solution.py:10
  151.2 9.8 %collective-permute-start = (f32[64,1024]{1,0:T(8,128)S(1)}, f32[64,1024]{1,0:T(8,128)S(1)}, u32[]{:S(2)}, u32[]{:S(2)}) collective-permute-start(f32[64,1024]{1,0:T(8,128)S(1)} %get-tuple-element.202), channel_id=1, source_target_pairs={{4,0},{8,4},{12,8},{16,12},{20,16},{24,20},{28,24},{32,28},{36,32}... | collective-permute-start | bytes 786440 | tf_op jit(solution)/shard_map/while/body/eval_jaxpr/ppermute | solution.py:10
  161.0 9.8 %collective-permute-start = (f32[64,1024]{1,0:T(8,128)S(1)}, f32[64,1024]{1,0:T(8,128)S(1)}, u32[]{:S(2)}, u32[]{:S(2)}) collective-permute-start(f32[64,1024]{1,0:T(8,128)S(1)} %get-tuple-element.202), channel_id=1, source_target_pairs={{4,0},{8,4},{12,8},{16,12},{20,16},{24,20},{28,24},{32,28},{36,32}... | collective-permute-start | bytes 786440 | tf_op jit(solution)/shard_map/while/body/eval_jaxpr/ppermute | solution.py:10
  170.8 9.8 %collective-permute-start = (f32[64,1024]{1,0:T(8,128)S(1)}, f32[64,1024]{1,0:T(8,128)S(1)}, u32[]{:S(2)}, u32[]{:S(2)}) collective-permute-start(f32[64,1024]{1,0:T(8,128)S(1)} %get-tuple-element.202), channel_id=1, source_target_pairs={{4,0},{8,4},{12,8},{16,12},{20,16},{24,20},{28,24},{32,28},{36,32}... | collective-permute-start | bytes 786440 | tf_op jit(solution)/shard_map/while/body/eval_jaxpr/ppermute | solution.py:10
  180.6 9.8 %collective-permute-start = (f32[64,1024]{1,0:T(8,128)S(1)}, f32[64,1024]{1,0:T(8,128)S(1)}, u32[]{:S(2)}, u32[]{:S(2)}) collective-permute-start(f32[64,1024]{1,0:T(8,128)S(1)} %get-tuple-element.202), channel_id=1, source_target_pairs={{4,0},{8,4},{12,8},{16,12},{20,16},{24,20},{28,24},{32,28},{36,32}... | collective-permute-start | bytes 786440 | tf_op jit(solution)/shard_map/while/body/eval_jaxpr/ppermute | solution.py:10
  190.4 9.8 %collective-permute-start = (f32[64,1024]{1,0:T(8,128)S(1)}, f32[64,1024]{1,0:T(8,128)S(1)}, u32[]{:S(2)}, u32[]{:S(2)}) collective-permute-start(f32[64,1024]{1,0:T(8,128)S(1)} %get-tuple-element.202), channel_id=1, source_target_pairs={{4,0},{8,4},{12,8},{16,12},{20,16},{24,20},{28,24},{32,28},{36,32}... | collective-permute-start | bytes 786440 | tf_op jit(solution)/shard_map/while/body/eval_jaxpr/ppermute | solution.py:10
  200.2 9.8 %collective-permute-start = (f32[64,1024]{1,0:T(8,128)S(1)}, f32[64,1024]{1,0:T(8,128)S(1)}, u32[]{:S(2)}, u32[]{:S(2)}) collective-permute-start(f32[64,1024]{1,0:T(8,128)S(1)} %get-tuple-element.202), channel_id=1, source_target_pairs={{4,0},{8,4},{12,8},{16,12},{20,16},{24,20},{28,24},{32,28},{36,32}... | collective-permute-start | bytes 786440 | tf_op jit(solution)/shard_map/while/body/eval_jaxpr/ppermute | solution.py:10
  209.9 9.8 %collective-permute-start = (f32[64,1024]{1,0:T(8,128)S(1)}, f32[64,1024]{1,0:T(8,128)S(1)}, u32[]{:S(2)}, u32[]{:S(2)}) collective-permute-start(f32[64,1024]{1,0:T(8,128)S(1)} %get-tuple-element.202), channel_id=1, source_target_pairs={{4,0},{8,4},{12,8},{16,12},{20,16},{24,20},{28,24},{32,28},{36,32}... | collective-permute-start | bytes 786440 | tf_op jit(solution)/shard_map/while/body/eval_jaxpr/ppermute | solution.py:10
  219.7 9.8 %collective-permute-start = (f32[64,1024]{1,0:T(8,128)S(1)}, f32[64,1024]{1,0:T(8,128)S(1)}, u32[]{:S(2)}, u32[]{:S(2)}) collective-permute-start(f32[64,1024]{1,0:T(8,128)S(1)} %get-tuple-element.202), channel_id=1, source_target_pairs={{4,0},{8,4},{12,8},{16,12},{20,16},{24,20},{28,24},{32,28},{36,32}... | collective-permute-start | bytes 786440 | tf_op jit(solution)/shard_map/while/body/eval_jaxpr/ppermute | solution.py:10
  229.5 9.8 %collective-permute-start = (f32[64,1024]{1,0:T(8,128)S(1)}, f32[64,1024]{1,0:T(8,128)S(1)}, u32[]{:S(2)}, u32[]{:S(2)}) collective-permute-start(f32[64,1024]{1,0:T(8,128)S(1)} %get-tuple-element.202), channel_id=1, source_target_pairs={{4,0},{8,4},{12,8},{16,12},{20,16},{24,20},{28,24},{32,28},{36,32}... | collective-permute-start | bytes 786440 | tf_op jit(solution)/shard_map/while/body/eval_jaxpr/ppermute | solution.py:10
  239.3 9.8 %collective-permute-start = (f32[64,1024]{1,0:T(8,128)S(1)}, f32[64,1024]{1,0:T(8,128)S(1)}, u32[]{:S(2)}, u32[]{:S(2)}) collective-permute-start(f32[64,1024]{1,0:T(8,128)S(1)} %get-tuple-element.202), channel_id=1, source_target_pairs={{4,0},{8,4},{12,8},{16,12},{20,16},{24,20},{28,24},{32,28},{36,32}... | collective-permute-start | bytes 786440 | tf_op jit(solution)/shard_map/while/body/eval_jaxpr/ppermute | solution.py:10
  249.1 9.8 %collective-permute-start = (f32[64,1024]{1,0:T(8,128)S(1)}, f32[64,1024]{1,0:T(8,128)S(1)}, u32[]{:S(2)}, u32[]{:S(2)}) collective-permute-start(f32[64,1024]{1,0:T(8,128)S(1)} %get-tuple-element.202), channel_id=1, source_target_pairs={{4,0},{8,4},{12,8},{16,12},{20,16},{24,20},{28,24},{32,28},{36,32}... | collective-permute-start | bytes 786440 | tf_op jit(solution)/shard_map/while/body/eval_jaxpr/ppermute | solution.py:10
  258.9 9.8 %collective-permute-start = (f32[64,1024]{1,0:T(8,128)S(1)}, f32[64,1024]{1,0:T(8,128)S(1)}, u32[]{:S(2)}, u32[]{:S(2)}) collective-permute-start(f32[64,1024]{1,0:T(8,128)S(1)} %get-tuple-element.202), channel_id=1, source_target_pairs={{4,0},{8,4},{12,8},{16,12},{20,16},{24,20},{28,24},{32,28},{36,32}... | collective-permute-start | bytes 786440 | tf_op jit(solution)/shard_map/while/body/eval_jaxpr/ppermute | solution.py:10
  268.7 9.8 %collective-permute-start = (f32[64,1024]{1,0:T(8,128)S(1)}, f32[64,1024]{1,0:T(8,128)S(1)}, u32[]{:S(2)}, u32[]{:S(2)}) collective-permute-start(f32[64,1024]{1,0:T(8,128)S(1)} %get-tuple-element.202), channel_id=1, source_target_pairs={{4,0},{8,4},{12,8},{16,12},{20,16},{24,20},{28,24},{32,28},{36,32}... | collective-permute-start | bytes 786440 | tf_op jit(solution)/shard_map/while/body/eval_jaxpr/ppermute | solution.py:10
  278.5 9.8 %collective-permute-start = (f32[64,1024]{1,0:T(8,128)S(1)}, f32[64,1024]{1,0:T(8,128)S(1)}, u32[]{:S(2)}, u32[]{:S(2)}) collective-permute-start(f32[64,1024]{1,0:T(8,128)S(1)} %get-tuple-element.202), channel_id=1, source_target_pairs={{4,0},{8,4},{12,8},{16,12},{20,16},{24,20},{28,24},{32,28},{36,32}... | collective-permute-start | bytes 786440 | tf_op jit(solution)/shard_map/while/body/eval_jaxpr/ppermute | solution.py:10
  288.3 9.8 %collective-permute-start = (f32[64,1024]{1,0:T(8,128)S(1)}, f32[64,1024]{1,0:T(8,128)S(1)}, u32[]{:S(2)}, u32[]{:S(2)}) collective-permute-start(f32[64,1024]{1,0:T(8,128)S(1)} %get-tuple-element.202), channel_id=1, source_target_pairs={{4,0},{8,4},{12,8},{16,12},{20,16},{24,20},{28,24},{32,28},{36,32}... | collective-permute-start | bytes 786440 | tf_op jit(solution)/shard_map/while/body/eval_jaxpr/ppermute | solution.py:10
  298.1 9.8 %collective-permute-start = (f32[64,1024]{1,0:T(8,128)S(1)}, f32[64,1024]{1,0:T(8,128)S(1)}, u32[]{:S(2)}, u32[]{:S(2)}) collective-permute-start(f32[64,1024]{1,0:T(8,128)S(1)} %get-tuple-element.202), channel_id=1, source_target_pairs={{4,0},{8,4},{12,8},{16,12},{20,16},{24,20},{28,24},{32,28},{36,32}... | collective-permute-start | bytes 786440 | tf_op jit(solution)/shard_map/while/body/eval_jaxpr/ppermute | solution.py:10
  307.8 9.8 %collective-permute-start = (f32[64,1024]{1,0:T(8,128)S(1)}, f32[64,1024]{1,0:T(8,128)S(1)}, u32[]{:S(2)}, u32[]{:S(2)}) collective-permute-start(f32[64,1024]{1,0:T(8,128)S(1)} %get-tuple-element.202), channel_id=1, source_target_pairs={{4,0},{8,4},{12,8},{16,12},{20,16},{24,20},{28,24},{32,28},{36,32}... | collective-permute-start | bytes 786440 | tf_op jit(solution)/shard_map/while/body/eval_jaxpr/ppermute | solution.py:10
  317.6 9.8 %collective-permute-start = (f32[64,1024]{1,0:T(8,128)S(1)}, f32[64,1024]{1,0:T(8,128)S(1)}, u32[]{:S(2)}, u32[]{:S(2)}) collective-permute-start(f32[64,1024]{1,0:T(8,128)S(1)} %get-tuple-element.202), channel_id=1, source_target_pairs={{4,0},{8,4},{12,8},{16,12},{20,16},{24,20},{28,24},{32,28},{36,32}... | collective-permute-start | bytes 786440 | tf_op jit(solution)/shard_map/while/body/eval_jaxpr/ppermute | solution.py:10
  327.4 9.8 %collective-permute-start = (f32[64,1024]{1,0:T(8,128)S(1)}, f32[64,1024]{1,0:T(8,128)S(1)}, u32[]{:S(2)}, u32[]{:S(2)}) collective-permute-start(f32[64,1024]{1,0:T(8,128)S(1)} %get-tuple-element.202), channel_id=1, source_target_pairs={{4,0},{8,4},{12,8},{16,12},{20,16},{24,20},{28,24},{32,28},{36,32}... | collective-permute-start | bytes 786440 | tf_op jit(solution)/shard_map/while/body/eval_jaxpr/ppermute | solution.py:10
  337.2 9.8 %collective-permute-start = (f32[64,1024]{1,0:T(8,128)S(1)}, f32[64,1024]{1,0:T(8,128)S(1)}, u32[]{:S(2)}, u32[]{:S(2)}) collective-permute-start(f32[64,1024]{1,0:T(8,128)S(1)} %get-tuple-element.202), channel_id=1, source_target_pairs={{4,0},{8,4},{12,8},{16,12},{20,16},{24,20},{28,24},{32,28},{36,32}... | collective-permute-start | bytes 786440 | tf_op jit(solution)/shard_map/while/body/eval_jaxpr/ppermute | solution.py:10
  347.0 9.8 %collective-permute-start = (f32[64,1024]{1,0:T(8,128)S(1)}, f32[64,1024]{1,0:T(8,128)S(1)}, u32[]{:S(2)}, u32[]{:S(2)}) collective-permute-start(f32[64,1024]{1,0:T(8,128)S(1)} %get-tuple-element.202), channel_id=1, source_target_pairs={{4,0},{8,4},{12,8},{16,12},{20,16},{24,20},{28,24},{32,28},{36,32}... | collective-permute-start | bytes 786440 | tf_op jit(solution)/shard_map/while/body/eval_jaxpr/ppermute | solution.py:10
  356.8 9.8 %collective-permute-start = (f32[64,1024]{1,0:T(8,128)S(1)}, f32[64,1024]{1,0:T(8,128)S(1)}, u32[]{:S(2)}, u32[]{:S(2)}) collective-permute-start(f32[64,1024]{1,0:T(8,128)S(1)} %get-tuple-element.202), channel_id=1, source_target_pairs={{4,0},{8,4},{12,8},{16,12},{20,16},{24,20},{28,24},{32,28},{36,32}... | collective-permute-start | bytes 786440 | tf_op jit(solution)/shard_map/while/body/eval_jaxpr/ppermute | solution.py:10
  366.6 9.8 %collective-permute-start = (f32[64,1024]{1,0:T(8,128)S(1)}, f32[64,1024]{1,0:T(8,128)S(1)}, u32[]{:S(2)}, u32[]{:S(2)}) collective-permute-start(f32[64,1024]{1,0:T(8,128)S(1)} %get-tuple-element.202), channel_id=1, source_target_pairs={{4,0},{8,4},{12,8},{16,12},{20,16},{24,20},{28,24},{32,28},{36,32}... | collective-permute-start | bytes 786440 | tf_op jit(solution)/shard_map/while/body/eval_jaxpr/ppermute | solution.py:10
  376.4 9.8 %collective-permute-start = (f32[64,1024]{1,0:T(8,128)S(1)}, f32[64,1024]{1,0:T(8,128)S(1)}, u32[]{:S(2)}, u32[]{:S(2)}) collective-permute-start(f32[64,1024]{1,0:T(8,128)S(1)} %get-tuple-element.202), channel_id=1, source_target_pairs={{4,0},{8,4},{12,8},{16,12},{20,16},{24,20},{28,24},{32,28},{36,32}... | collective-permute-start | bytes 786440 | tf_op jit(solution)/shard_map/while/body/eval_jaxpr/ppermute | solution.py:10
  386.2 9.8 %collective-permute-start = (f32[64,1024]{1,0:T(8,128)S(1)}, f32[64,1024]{1,0:T(8,128)S(1)}, u32[]{:S(2)}, u32[]{:S(2)}) collective-permute-start(f32[64,1024]{1,0:T(8,128)S(1)} %get-tuple-element.202), channel_id=1, source_target_pairs={{4,0},{8,4},{12,8},{16,12},{20,16},{24,20},{28,24},{32,28},{36,32}... | collective-permute-start | bytes 786440 | tf_op jit(solution)/shard_map/while/body/eval_jaxpr/ppermute | solution.py:10
  396.0 9.8 %collective-permute-start = (f32[64,1024]{1,0:T(8,128)S(1)}, f32[64,1024]{1,0:T(8,128)S(1)}, u32[]{:S(2)}, u32[]{:S(2)}) collective-permute-start(f32[64,1024]{1,0:T(8,128)S(1)} %get-tuple-element.202), channel_id=1, source_target_pairs={{4,0},{8,4},{12,8},{16,12},{20,16},{24,20},{28,24},{32,28},{36,32}... | collective-permute-start | bytes 786440 | tf_op jit(solution)/shard_map/while/body/eval_jaxpr/ppermute | solution.py:10
  572.2 86.0 %collective-permute-start = (f32[64,1024]{1,0:T(8,128)S(1)}, f32[64,1024]{1,0:T(8,128)S(1)}, u32[]{:S(2)}, u32[]{:S(2)}) collective-permute-start(f32[64,1024]{1,0:T(8,128)S(1)} %get-tuple-element.202), channel_id=1, source_target_pairs={{4,0},{8,4},{12,8},{16,12},{20,16},{24,20},{28,24},{32,28},{36,32}... | collective-permute-start | bytes 786440 | tf_op jit(solution)/shard_map/while/body/eval_jaxpr/ppermute | solution.py:10
  670.7 116.7 %collective-permute-start.1 = (f32[64,1024]{1,0:T(8,128)S(1)}, f32[64,1024]{1,0:T(8,128)S(1)}, u32[]{:S(2)}, u32[]{:S(2)}) collective-permute-start(f32[64,1024]{1,0:T(8,128)S(1)} %get-tuple-element.150), channel_id=1, source_target_pairs={{4,0},{8,4},{12,8},{16,12},{20,16},{24,20},{28,24},{32,28},{36,32}... | collective-permute-start | bytes 786440 | tf_op jit(solution)/shard_map/ppermute | solution.py:10
  (35 other events, 1635.1 us)
where the time goes:
time: 793 us; the launch traced here: 791 us
  waiting for transfers between devices  540 us (68%)
  starting transfers between devices  126 us (16%)
  blocking collectives  108 us (14%)
  matrix products  13.4 us (2%)
    ppermute x64, waiting for transfers between devices, from_behind(): return lax.ppermute(array, axis, pairs)  540 us
    ppermute x64, starting transfers between devices, from_behind(): return lax.ppermute(array, axis, pairs)  126 us
    psum x1, blocking collectives, local(): corner = corner_base + lax.psum(partial_value, ('tm', 'col'))  108 us
  transfers between devices with their start and end apart: 64, of which 63 were waited for; matrix products, arithmetic and copies ran while one was open for 1% of the time, Pallas kernels for 0%

commit v1 on v0

--- a/solution.py
+++ b/solution.py
@@ -50,7 +50,7 @@
     partial_value = jnp.dot(
         arrow_rows[0], own_columns.T, precision=highest, preferred_element_type=jnp.float32
     )
-    corner = corner_base + lax.psum(partial_value, ("tm", "col"))
+    corner = corner_base + jnp.sum(lax.all_gather(partial_value, ("tm", "col")), axis=0)
     return (own_columns[None], slab_blocks[None], corner)
 
 

time: 793 us -> 840 us (1.059)
  waiting for transfers between devices: 540 us -> 676 us
  blocking collectives: 108 us -> 0 us
  between operations: 0.7 us -> 14.1 us
    all_gather x0 -> x1, waiting for transfers between devices: none -> 136 us  [local(): lax.all_gather(partial_value, ('tm', 'col'))]
    psum x1 -> x0, blocking collectives: 108 us -> none  [local(): corner = corner_base + lax.psum(partial_value, ('tm', 'col'))]
  transfers between devices with their start and end apart: 64 -> 65, of which waited for: 63 -> 64; matrix products, arithmetic and copies ran while one was open for 1% -> 1% of each run, Pallas kernels for 0% -> 0%
where the time goes in v1:
time: 840 us; the launch traced here: 838 us
  waiting for transfers between devices  676 us (80%)
  starting transfers between devices  126 us (15%)
  between operations  14.1 us (2%)
  matrix products  13.6 us (2%)
    ppermute x64, waiting for transfers between devices, from_behind(): return lax.ppermute(array, axis, pairs)  540 us
    all_gather x1, waiting for transfers between devices, local(): lax.all_gather(partial_value, ('tm', 'col'))  136 us
    ppermute x64, starting transfers between devices, from_behind(): return lax.ppermute(array, axis, pairs)  126 us
  transfers between devices with their start and end apart: 65, of which 64 were waited for; matrix products, arithmetic and copies ran while one was open for 1% of the time, Pallas kernels for 0%

profile of v1, /device:TPU:1, one launch (start us, length us, event | category | flops | bytes accessed | tf_op | source)
XLA Modules:
  0.0 838.1 jit_solution(9417791552201935555)
XLA Ops:
  8.2 669.1 %while.18 = (s32[]{:T(128)}, f32[64,1024]{1,0:T(8,128)S(1)}, s32[]{:T(128)}, f32[1024,1024]{1,0:T(8,128)}, f32[64,1024]{1,0:T(8,128)}, /*index=5*/s32[]{:T(128)}) while((s32[]{:T(128)}, f32[64,1024]{1,0:T(8,128)S(1)}, s32[]{:T(128)}, f32[1024,1024]{1,0:T(8,128)}, f32[64,1024]{1,0:T(8,128)}, /*index=5*/s32[]{:T(128)}) %tuple.62), condition=%wide.region_3.0_spmd, body=%wide.region_0.0_spmd.sunk | while | flops 805371904 | bytes 6029467 | solution.py:37
  120.5 7.9 collective-permute-done
  130.3 7.9 collective-permute-done
  140.1 7.9 collective-permute-done
  149.9 7.9 collective-permute-done
  159.7 7.9 collective-permute-done
  169.5 7.9 collective-permute-done
  179.3 7.9 collective-permute-done
  189.0 7.9 collective-permute-done
  198.8 7.9 collective-permute-done
  208.6 7.9 collective-permute-done
  218.4 7.9 collective-permute-done
  228.2 7.9 collective-permute-done
  238.0 7.9 collective-permute-done
  247.8 7.9 collective-permute-done
  257.6 7.9 collective-permute-done
  267.4 7.9 collective-permute-done
  277.2 7.9 collective-permute-done
  286.9 7.9 collective-permute-done
  296.7 7.9 collective-permute-done
  306.5 7.9 collective-permute-done
  316.3 7.9 collective-permute-done
  326.1 7.9 collective-permute-done
  335.9 7.9 collective-permute-done
  345.7 7.9 collective-permute-done
  355.5 7.9 collective-permute-done
  365.3 7.9 collective-permute-done
  375.1 7.9 collective-permute-done
  384.8 7.9 collective-permute-done
  394.6 7.9 collective-permute-done
  580.6 84.1 %collective-permute-done = f32[64,1024]{1,0:T(8,128)S(1)} collective-permute-done((f32[64,1024]{1,0:T(8,128)S(1)}, f32[64,1024]{1,0:T(8,128)S(1)}, u32[]{:S(2)}, u32[]{:S(2)}) %collective-permute-start) | collective-permute-done | bytes 262176 | tf_op jit(solution)/shard_map/while/body/eval_jaxpr/ppermute | solution.py:10
  690.1 136.4 %all-gather.3.cloned.1.call-done = f32[16384,64]{1,0:T(8,128)} async-done(((f32[64,64]{1,0:T(8,128)}), f32[16384,64]{1,0:T(8,128)}) %all-gather.3.cloned.1.call-update) | async-done | bytes 4194320 | tf_op jit(solution)/shard_map/all_gather | solution.py:53
  (181 shorter events, 379.3 us)
Async XLA Ops:
  7.2 819.3 %all-gather.3.cloned.1.call-start = ((), (), s32[]{:S(2)}) async-start(), calls=%async_computation | async-start | bytes 8421376 | tf_op jit(solution)/shard_map/all_gather | solution.py:53
  118.6 9.8 %collective-permute-start = (f32[64,1024]{1,0:T(8,128)S(1)}, f32[64,1024]{1,0:T(8,128)S(1)}, u32[]{:S(2)}, u32[]{:S(2)}) collective-permute-start(f32[64,1024]{1,0:T(8,128)S(1)} %get-tuple-element.202), channel_id=1, source_target_pairs={{4,0},{8,4},{12,8},{16,12},{20,16},{24,20},{28,24},{32,28},{36,32}... | collective-permute-start | bytes 786440 | tf_op jit(solution)/shard_map/while/body/eval_jaxpr/ppermute | solution.py:10
  128.4 9.8 %collective-permute-start = (f32[64,1024]{1,0:T(8,128)S(1)}, f32[64,1024]{1,0:T(8,128)S(1)}, u32[]{:S(2)}, u32[]{:S(2)}) collective-permute-start(f32[64,1024]{1,0:T(8,128)S(1)} %get-tuple-element.202), channel_id=1, source_target_pairs={{4,0},{8,4},{12,8},{16,12},{20,16},{24,20},{28,24},{32,28},{36,32}... | collective-permute-start | bytes 786440 | tf_op jit(solution)/shard_map/while/body/eval_jaxpr/ppermute | solution.py:10
  138.2 9.8 %collective-permute-start = (f32[64,1024]{1,0:T(8,128)S(1)}, f32[64,1024]{1,0:T(8,128)S(1)}, u32[]{:S(2)}, u32[]{:S(2)}) collective-permute-start(f32[64,1024]{1,0:T(8,128)S(1)} %get-tuple-element.202), channel_id=1, source_target_pairs={{4,0},{8,4},{12,8},{16,12},{20,16},{24,20},{28,24},{32,28},{36,32}... | collective-permute-start | bytes 786440 | tf_op jit(solution)/shard_map/while/body/eval_jaxpr/ppermute | solution.py:10
  148.0 9.8 %collective-permute-start = (f32[64,1024]{1,0:T(8,128)S(1)}, f32[64,1024]{1,0:T(8,128)S(1)}, u32[]{:S(2)}, u32[]{:S(2)}) collective-permute-start(f32[64,1024]{1,0:T(8,128)S(1)} %get-tuple-element.202), channel_id=1, source_target_pairs={{4,0},{8,4},{12,8},{16,12},{20,16},{24,20},{28,24},{32,28},{36,32}... | collective-permute-start | bytes 786440 | tf_op jit(solution)/shard_map/while/body/eval_jaxpr/ppermute | solution.py:10
  157.8 9.8 %collective-permute-start = (f32[64,1024]{1,0:T(8,128)S(1)}, f32[64,1024]{1,0:T(8,128)S(1)}, u32[]{:S(2)}, u32[]{:S(2)}) collective-permute-start(f32[64,1024]{1,0:T(8,128)S(1)} %get-tuple-element.202), channel_id=1, source_target_pairs={{4,0},{8,4},{12,8},{16,12},{20,16},{24,20},{28,24},{32,28},{36,32}... | collective-permute-start | bytes 786440 | tf_op jit(solution)/shard_map/while/body/eval_jaxpr/ppermute | solution.py:10
  167.5 9.8 %collective-permute-start = (f32[64,1024]{1,0:T(8,128)S(1)}, f32[64,1024]{1,0:T(8,128)S(1)}, u32[]{:S(2)}, u32[]{:S(2)}) collective-permute-start(f32[64,1024]{1,0:T(8,128)S(1)} %get-tuple-element.202), channel_id=1, source_target_pairs={{4,0},{8,4},{12,8},{16,12},{20,16},{24,20},{28,24},{32,28},{36,32}... | collective-permute-start | bytes 786440 | tf_op jit(solution)/shard_map/while/body/eval_jaxpr/ppermute | solution.py:10
  177.3 9.8 %collective-permute-start = (f32[64,1024]{1,0:T(8,128)S(1)}, f32[64,1024]{1,0:T(8,128)S(1)}, u32[]{:S(2)}, u32[]{:S(2)}) collective-permute-start(f32[64,1024]{1,0:T(8,128)S(1)} %get-tuple-element.202), channel_id=1, source_target_pairs={{4,0},{8,4},{12,8},{16,12},{20,16},{24,20},{28,24},{32,28},{36,32}... | collective-permute-start | bytes 786440 | tf_op jit(solution)/shard_map/while/body/eval_jaxpr/ppermute | solution.py:10
  187.1 9.8 %collective-permute-start = (f32[64,1024]{1,0:T(8,128)S(1)}, f32[64,1024]{1,0:T(8,128)S(1)}, u32[]{:S(2)}, u32[]{:S(2)}) collective-permute-start(f32[64,1024]{1,0:T(8,128)S(1)} %get-tuple-element.202), channel_id=1, source_target_pairs={{4,0},{8,4},{12,8},{16,12},{20,16},{24,20},{28,24},{32,28},{36,32}... | collective-permute-start | bytes 786440 | tf_op jit(solution)/shard_map/while/body/eval_jaxpr/ppermute | solution.py:10
  196.9 9.8 %collective-permute-start = (f32[64,1024]{1,0:T(8,128)S(1)}, f32[64,1024]{1,0:T(8,128)S(1)}, u32[]{:S(2)}, u32[]{:S(2)}) collective-permute-start(f32[64,1024]{1,0:T(8,128)S(1)} %get-tuple-element.202), channel_id=1, source_target_pairs={{4,0},{8,4},{12,8},{16,12},{20,16},{24,20},{28,24},{32,28},{36,32}... | collective-permute-start | bytes 786440 | tf_op jit(solution)/shard_map/while/body/eval_jaxpr/ppermute | solution.py:10
  206.7 9.8 %collective-permute-start = (f32[64,1024]{1,0:T(8,128)S(1)}, f32[64,1024]{1,0:T(8,128)S(1)}, u32[]{:S(2)}, u32[]{:S(2)}) collective-permute-start(f32[64,1024]{1,0:T(8,128)S(1)} %get-tuple-element.202), channel_id=1, source_target_pairs={{4,0},{8,4},{12,8},{16,12},{20,16},{24,20},{28,24},{32,28},{36,32}... | collective-permute-start | bytes 786440 | tf_op jit(solution)/shard_map/while/body/eval_jaxpr/ppermute | solution.py:10
  216.5 9.8 %collective-permute-start = (f32[64,1024]{1,0:T(8,128)S(1)}, f32[64,1024]{1,0:T(8,128)S(1)}, u32[]{:S(2)}, u32[]{:S(2)}) collective-permute-start(f32[64,1024]{1,0:T(8,128)S(1)} %get-tuple-element.202), channel_id=1, source_target_pairs={{4,0},{8,4},{12,8},{16,12},{20,16},{24,20},{28,24},{32,28},{36,32}... | collective-permute-start | bytes 786440 | tf_op jit(solution)/shard_map/while/body/eval_jaxpr/ppermute | solution.py:10
  226.3 9.8 %collective-permute-start = (f32[64,1024]{1,0:T(8,128)S(1)}, f32[64,1024]{1,0:T(8,128)S(1)}, u32[]{:S(2)}, u32[]{:S(2)}) collective-permute-start(f32[64,1024]{1,0:T(8,128)S(1)} %get-tuple-element.202), channel_id=1, source_target_pairs={{4,0},{8,4},{12,8},{16,12},{20,16},{24,20},{28,24},{32,28},{36,32}... | collective-permute-start | bytes 786440 | tf_op jit(solution)/shard_map/while/body/eval_jaxpr/ppermute | solution.py:10
  236.1 9.8 %collective-permute-start = (f32[64,1024]{1,0:T(8,128)S(1)}, f32[64,1024]{1,0:T(8,128)S(1)}, u32[]{:S(2)}, u32[]{:S(2)}) collective-permute-start(f32[64,1024]{1,0:T(8,128)S(1)} %get-tuple-element.202), channel_id=1, source_target_pairs={{4,0},{8,4},{12,8},{16,12},{20,16},{24,20},{28,24},{32,28},{36,32}... | collective-permute-start | bytes 786440 | tf_op jit(solution)/shard_map/while/body/eval_jaxpr/ppermute | solution.py:10
  245.9 9.8 %collective-permute-start = (f32[64,1024]{1,0:T(8,128)S(1)}, f32[64,1024]{1,0:T(8,128)S(1)}, u32[]{:S(2)}, u32[]{:S(2)}) collective-permute-start(f32[64,1024]{1,0:T(8,128)S(1)} %get-tuple-element.202), channel_id=1, source_target_pairs={{4,0},{8,4},{12,8},{16,12},{20,16},{24,20},{28,24},{32,28},{36,32}... | collective-permute-start | bytes 786440 | tf_op jit(solution)/shard_map/while/body/eval_jaxpr/ppermute | solution.py:10
  255.7 9.8 %collective-permute-start = (f32[64,1024]{1,0:T(8,128)S(1)}, f32[64,1024]{1,0:T(8,128)S(1)}, u32[]{:S(2)}, u32[]{:S(2)}) collective-permute-start(f32[64,1024]{1,0:T(8,128)S(1)} %get-tuple-element.202), channel_id=1, source_target_pairs={{4,0},{8,4},{12,8},{16,12},{20,16},{24,20},{28,24},{32,28},{36,32}... | collective-permute-start | bytes 786440 | tf_op jit(solution)/shard_map/while/body/eval_jaxpr/ppermute | solution.py:10
  265.4 9.8 %collective-permute-start = (f32[64,1024]{1,0:T(8,128)S(1)}, f32[64,1024]{1,0:T(8,128)S(1)}, u32[]{:S(2)}, u32[]{:S(2)}) collective-permute-start(f32[64,1024]{1,0:T(8,128)S(1)} %get-tuple-element.202), channel_id=1, source_target_pairs={{4,0},{8,4},{12,8},{16,12},{20,16},{24,20},{28,24},{32,28},{36,32}... | collective-permute-start | bytes 786440 | tf_op jit(solution)/shard_map/while/body/eval_jaxpr/ppermute | solution.py:10
  275.2 9.8 %collective-permute-start = (f32[64,1024]{1,0:T(8,128)S(1)}, f32[64,1024]{1,0:T(8,128)S(1)}, u32[]{:S(2)}, u32[]{:S(2)}) collective-permute-start(f32[64,1024]{1,0:T(8,128)S(1)} %get-tuple-element.202), channel_id=1, source_target_pairs={{4,0},{8,4},{12,8},{16,12},{20,16},{24,20},{28,24},{32,28},{36,32}... | collective-permute-start | bytes 786440 | tf_op jit(solution)/shard_map/while/body/eval_jaxpr/ppermute | solution.py:10
  285.0 9.8 %collective-permute-start = (f32[64,1024]{1,0:T(8,128)S(1)}, f32[64,1024]{1,0:T(8,128)S(1)}, u32[]{:S(2)}, u32[]{:S(2)}) collective-permute-start(f32[64,1024]{1,0:T(8,128)S(1)} %get-tuple-element.202), channel_id=1, source_target_pairs={{4,0},{8,4},{12,8},{16,12},{20,16},{24,20},{28,24},{32,28},{36,32}... | collective-permute-start | bytes 786440 | tf_op jit(solution)/shard_map/while/body/eval_jaxpr/ppermute | solution.py:10
  294.8 9.8 %collective-permute-start = (f32[64,1024]{1,0:T(8,128)S(1)}, f32[64,1024]{1,0:T(8,128)S(1)}, u32[]{:S(2)}, u32[]{:S(2)}) collective-permute-start(f32[64,1024]{1,0:T(8,128)S(1)} %get-tuple-element.202), channel_id=1, source_target_pairs={{4,0},{8,4},{12,8},{16,12},{20,16},{24,20},{28,24},{32,28},{36,32}... | collective-permute-start | bytes 786440 | tf_op jit(solution)/shard_map/while/body/eval_jaxpr/ppermute | solution.py:10
  304.6 9.8 %collective-permute-start = (f32[64,1024]{1,0:T(8,128)S(1)}, f32[64,1024]{1,0:T(8,128)S(1)}, u32[]{:S(2)}, u32[]{:S(2)}) collective-permute-start(f32[64,1024]{1,0:T(8,128)S(1)} %get-tuple-element.202), channel_id=1, source_target_pairs={{4,0},{8,4},{12,8},{16,12},{20,16},{24,20},{28,24},{32,28},{36,32}... | collective-permute-start | bytes 786440 | tf_op jit(solution)/shard_map/while/body/eval_jaxpr/ppermute | solution.py:10
  314.4 9.8 %collective-permute-start = (f32[64,1024]{1,0:T(8,128)S(1)}, f32[64,1024]{1,0:T(8,128)S(1)}, u32[]{:S(2)}, u32[]{:S(2)}) collective-permute-start(f32[64,1024]{1,0:T(8,128)S(1)} %get-tuple-element.202), channel_id=1, source_target_pairs={{4,0},{8,4},{12,8},{16,12},{20,16},{24,20},{28,24},{32,28},{36,32}... | collective-permute-start | bytes 786440 | tf_op jit(solution)/shard_map/while/body/eval_jaxpr/ppermute | solution.py:10
  324.2 9.8 %collective-permute-start = (f32[64,1024]{1,0:T(8,128)S(1)}, f32[64,1024]{1,0:T(8,128)S(1)}, u32[]{:S(2)}, u32[]{:S(2)}) collective-permute-start(f32[64,1024]{1,0:T(8,128)S(1)} %get-tuple-element.202), channel_id=1, source_target_pairs={{4,0},{8,4},{12,8},{16,12},{20,16},{24,20},{28,24},{32,28},{36,32}... | collective-permute-start | bytes 786440 | tf_op jit(solution)/shard_map/while/body/eval_jaxpr/ppermute | solution.py:10
  334.0 9.8 %collective-permute-start = (f32[64,1024]{1,0:T(8,128)S(1)}, f32[64,1024]{1,0:T(8,128)S(1)}, u32[]{:S(2)}, u32[]{:S(2)}) collective-permute-start(f32[64,1024]{1,0:T(8,128)S(1)} %get-tuple-element.202), channel_id=1, source_target_pairs={{4,0},{8,4},{12,8},{16,12},{20,16},{24,20},{28,24},{32,28},{36,32}... | collective-permute-start | bytes 786440 | tf_op jit(solution)/shard_map/while/body/eval_jaxpr/ppermute | solution.py:10
  343.8 9.8 %collective-permute-start = (f32[64,1024]{1,0:T(8,128)S(1)}, f32[64,1024]{1,0:T(8,128)S(1)}, u32[]{:S(2)}, u32[]{:S(2)}) collective-permute-start(f32[64,1024]{1,0:T(8,128)S(1)} %get-tuple-element.202), channel_id=1, source_target_pairs={{4,0},{8,4},{12,8},{16,12},{20,16},{24,20},{28,24},{32,28},{36,32}... | collective-permute-start | bytes 786440 | tf_op jit(solution)/shard_map/while/body/eval_jaxpr/ppermute | solution.py:10
  353.6 9.8 %collective-permute-start = (f32[64,1024]{1,0:T(8,128)S(1)}, f32[64,1024]{1,0:T(8,128)S(1)}, u32[]{:S(2)}, u32[]{:S(2)}) collective-permute-start(f32[64,1024]{1,0:T(8,128)S(1)} %get-tuple-element.202), channel_id=1, source_target_pairs={{4,0},{8,4},{12,8},{16,12},{20,16},{24,20},{28,24},{32,28},{36,32}... | collective-permute-start | bytes 786440 | tf_op jit(solution)/shard_map/while/body/eval_jaxpr/ppermute | solution.py:10
  363.3 9.8 %collective-permute-start = (f32[64,1024]{1,0:T(8,128)S(1)}, f32[64,1024]{1,0:T(8,128)S(1)}, u32[]{:S(2)}, u32[]{:S(2)}) collective-permute-start(f32[64,1024]{1,0:T(8,128)S(1)} %get-tuple-element.202), channel_id=1, source_target_pairs={{4,0},{8,4},{12,8},{16,12},{20,16},{24,20},{28,24},{32,28},{36,32}... | collective-permute-start | bytes 786440 | tf_op jit(solution)/shard_map/while/body/eval_jaxpr/ppermute | solution.py:10
  373.1 9.8 %collective-permute-start = (f32[64,1024]{1,0:T(8,128)S(1)}, f32[64,1024]{1,0:T(8,128)S(1)}, u32[]{:S(2)}, u32[]{:S(2)}) collective-permute-start(f32[64,1024]{1,0:T(8,128)S(1)} %get-tuple-element.202), channel_id=1, source_target_pairs={{4,0},{8,4},{12,8},{16,12},{20,16},{24,20},{28,24},{32,28},{36,32}... | collective-permute-start | bytes 786440 | tf_op jit(solution)/shard_map/while/body/eval_jaxpr/ppermute | solution.py:10
  382.9 9.8 %collective-permute-start = (f32[64,1024]{1,0:T(8,128)S(1)}, f32[64,1024]{1,0:T(8,128)S(1)}, u32[]{:S(2)}, u32[]{:S(2)}) collective-permute-start(f32[64,1024]{1,0:T(8,128)S(1)} %get-tuple-element.202), channel_id=1, source_target_pairs={{4,0},{8,4},{12,8},{16,12},{20,16},{24,20},{28,24},{32,28},{36,32}... | collective-permute-start | bytes 786440 | tf_op jit(solution)/shard_map/while/body/eval_jaxpr/ppermute | solution.py:10
  392.7 9.8 %collective-permute-start = (f32[64,1024]{1,0:T(8,128)S(1)}, f32[64,1024]{1,0:T(8,128)S(1)}, u32[]{:S(2)}, u32[]{:S(2)}) collective-permute-start(f32[64,1024]{1,0:T(8,128)S(1)} %get-tuple-element.202), channel_id=1, source_target_pairs={{4,0},{8,4},{12,8},{16,12},{20,16},{24,20},{28,24},{32,28},{36,32}... | collective-permute-start | bytes 786440 | tf_op jit(solution)/shard_map/while/body/eval_jaxpr/ppermute | solution.py:10
  402.5 9.8 %collective-permute-start = (f32[64,1024]{1,0:T(8,128)S(1)}, f32[64,1024]{1,0:T(8,128)S(1)}, u32[]{:S(2)}, u32[]{:S(2)}) collective-permute-start(f32[64,1024]{1,0:T(8,128)S(1)} %get-tuple-element.202), channel_id=1, source_target_pairs={{4,0},{8,4},{12,8},{16,12},{20,16},{24,20},{28,24},{32,28},{36,32}... | collective-permute-start | bytes 786440 | tf_op jit(solution)/shard_map/while/body/eval_jaxpr/ppermute | solution.py:10
  578.7 86.0 %collective-permute-start = (f32[64,1024]{1,0:T(8,128)S(1)}, f32[64,1024]{1,0:T(8,128)S(1)}, u32[]{:S(2)}, u32[]{:S(2)}) collective-permute-start(f32[64,1024]{1,0:T(8,128)S(1)} %get-tuple-element.202), channel_id=1, source_target_pairs={{4,0},{8,4},{12,8},{16,12},{20,16},{24,20},{28,24},{32,28},{36,32}... | collective-permute-start | bytes 786440 | tf_op jit(solution)/shard_map/while/body/eval_jaxpr/ppermute | solution.py:10
  (36 other events, 1641.5 us)
Sparse Core Ops, SparseCore 0:
  678.3 148.0 all-gather.2
